TPU v7x, 32 devices: a whole 2x2x4 slice. The times are simulated.
32 devices in a mesh: rows: 16 (over z, y, core), cols: 2 (over x).
Axes of the slice: x: 2, y: 2, z: 4, core: 2. Of those that a mesh axis runs over, the one named last changes fastest.
Arguments:
- inputs: bfloat16 [96, 64, 640], P('rows', 'cols'), may hold values from -4 to 4
- qkv_weight: bfloat16 [640, 960], replicated, may hold values from -0.25 to 0.25
- out_weight: bfloat16 [320, 640], replicated, may hold values from -0.3125 to 0.3125
- attn_out: bfloat16 [96, 64, 320], P('rows', 'cols'), may hold values from -6 to 6
- log_norm: float32 [5, 96, 64], P(None, 'rows', 'cols'), may hold values from 4 to 6
- cotangent: bfloat16 [96, 64, 640], P('rows', 'cols'), may hold values from -6 to 6
Outputs:
- grad_input: bfloat16 [96, 64, 640], P('rows', 'cols')
- grad_qkv_weight: bfloat16 [640, 960], replicated
- grad_out_weight: bfloat16 [320, 640], replicated
All inputs are finite; a program needn't handle non-finite values.
Results may differ from a plain program's by a relative error of at most 0.01.
Values may be sent and summed in bfloat16 or wider, within the bound.
A program may use at most 64 MiB of HBM per device.

v0:
```python
import jax
import jax.numpy as jnp
from jax import lax
from jax.sharding import PartitionSpec as P

HEADS = 5
HEAD_DIM = 64
RADIUS = 6


def padded(block, sides, width):
    for axis, dim in sides:
        count = lax.axis_size(axis)
        forward = [(i, i + 1) for i in range(count - 1)]
        forward.append((count - 1, 0))
        backward = [(target, source) for source, target in forward]
        low = lax.ppermute(
            lax.slice_in_dim(block, block.shape[dim] - width, None, axis=dim), axis, forward
        )
        high = lax.ppermute(lax.slice_in_dim(block, 0, width, axis=dim), axis, backward)
        block = jnp.concatenate([low, block, high], axis=dim)
    return block


def window_mask(rows_dev, cols_dev, row_start, grid_rows):
    grown_cols = cols_dev + 2 * RADIUS
    grown_rows = rows_dev + 2 * RADIUS
    own_ids = jnp.arange(rows_dev * cols_dev)
    own_row = own_ids // cols_dev
    own_col = own_ids % cols_dev
    near_ids = jnp.arange(grown_rows * grown_cols)
    near_row = near_ids // grown_cols
    near_col = near_ids % grown_cols
    close_rows = jnp.abs(near_row[None, :] - RADIUS - own_row[:, None]) <= RADIUS
    close_cols = jnp.abs(near_col[None, :] - RADIUS - own_col[:, None]) <= RADIUS
    global_row = row_start + near_row - RADIUS
    in_grid = (global_row >= 0) & (global_row < grid_rows)
    return close_rows & close_cols & in_grid[None, :]


def shards(inputs, qkv_weight, out_weight, attn_out, log_norm, cotangent):
    rows_dev, cols_dev, model_width = inputs.shape
    tokens_dev = rows_dev * cols_dev
    inner_width = HEADS * HEAD_DIM
    score_scale = HEAD_DIM ** (-0.5)
    grown_rows = rows_dev + 2 * RADIUS
    grown_cols = cols_dev + 2 * RADIUS
    grown_tokens = grown_rows * grown_cols
    grid_tokens = tokens_dev * lax.axis_size("rows") * lax.axis_size("cols")
    grad_factor = grid_tokens ** (-0.5)
    flat_in = inputs.reshape(tokens_dev, model_width)
    flat_cot = cotangent.reshape(tokens_dev, model_width)
    flat_att = attn_out.reshape(tokens_dev, inner_width)
    projected = jnp.dot(flat_in, qkv_weight, preferred_element_type=jnp.float32).astype(
        jnp.bfloat16
    )
    grad_att = lax.dot_general(
        flat_cot, out_weight, (((1,), (1,)), ((), ())), preferred_element_type=jnp.float32
    ).astype(jnp.bfloat16)
    grad_wout = lax.dot_general(
        flat_att, flat_cot, (((0,), (0,)), ((), ())), preferred_element_type=jnp.float32
    )
    head_shape = (tokens_dev, HEADS, HEAD_DIM)
    queries = projected[:, :inner_width].reshape(head_shape)
    own_keyval = projected[:, inner_width:]
    upstream = grad_att.reshape(head_shape)
    row_delta = jnp.sum(
        upstream.astype(jnp.float32) * flat_att.reshape(head_shape).astype(jnp.float32), axis=2
    ).T
    own_norm = log_norm.reshape(HEADS, tokens_dev)
    inside = window_mask(
        rows_dev, cols_dev, lax.axis_index("rows") * rows_dev, rows_dev * lax.axis_size("rows")
    )
    block_keyval = own_keyval.reshape(rows_dev, cols_dev, 2 * inner_width)
    query_side = jnp.concatenate([projected[:, :inner_width], grad_att], axis=1).reshape(
        rows_dev, cols_dev, 2 * inner_width
    )
    near_keyval, near_qdo = (
        padded(block_keyval, (("rows", 0), ("cols", 1)), RADIUS),
        padded(query_side, (("rows", 0), ("cols", 1)), RADIUS),
    )
    own_stats = jnp.concatenate([own_norm, row_delta], axis=0).T.reshape(
        rows_dev, cols_dev, 2 * HEADS
    )
    near_stats = padded(own_stats, (("rows", 0), ("cols", 1)), RADIUS)
    flat_kv = near_keyval.reshape(grown_tokens, 2 * inner_width)
    near_keys = flat_kv[:, :inner_width].reshape(grown_tokens, HEADS, HEAD_DIM)
    near_values = flat_kv[:, inner_width:].reshape(grown_tokens, HEADS, HEAD_DIM)
    scores = (
        jnp.einsum("thd,ehd->hte", queries, near_keys, preferred_element_type=jnp.float32)
        * score_scale
    )
    weight = jnp.where(inside[None], jnp.exp(scores - own_norm[:, :, None]), 0.0)
    grad_weight = jnp.einsum(
        "thd,ehd->hte", upstream, near_values, preferred_element_type=jnp.float32
    )
    grad_score = (weight * (grad_weight - row_delta[:, :, None])).astype(jnp.bfloat16)
    grad_query = (
        jnp.einsum("hte,ehd->thd", grad_score, near_keys, preferred_element_type=jnp.float32)
        * score_scale
    )
    near_flat = near_qdo.reshape(grown_tokens, 2 * inner_width)
    near_queries = near_flat[:, :inner_width].reshape(grown_tokens, HEADS, HEAD_DIM)
    near_upstream = near_flat[:, inner_width:].reshape(grown_tokens, HEADS, HEAD_DIM)
    stats_flat = near_stats.reshape(grown_tokens, 2 * HEADS).T
    near_norm = stats_flat[:HEADS]
    near_delta = stats_flat[HEADS:]
    own_keys = own_keyval[:, :inner_width].reshape(head_shape)
    own_values = own_keyval[:, inner_width:].reshape(head_shape)
    scores_back = (
        jnp.einsum("ehd,thd->het", near_queries, own_keys, preferred_element_type=jnp.float32)
        * score_scale
    )
    weight_back = jnp.where(inside.T[None], jnp.exp(scores_back - near_norm[:, :, None]), 0.0)
    grad_back = jnp.einsum(
        "ehd,thd->het", near_upstream, own_values, preferred_element_type=jnp.float32
    )
    score_back_grad = (weight_back * (grad_back - near_delta[:, :, None])).astype(jnp.bfloat16)
    grad_keys = (
        jnp.einsum(
            "het,ehd->thd", score_back_grad, near_queries, preferred_element_type=jnp.float32
        )
        * score_scale
    )
    grad_values = jnp.einsum(
        "het,ehd->thd",
        weight_back.astype(jnp.bfloat16),
        near_upstream,
        preferred_element_type=jnp.float32,
    )
    grad_keyval = jnp.concatenate(
        [grad_keys.reshape(tokens_dev, inner_width), grad_values.reshape(tokens_dev, inner_width)],
        axis=1,
    )
    grad_proj = jnp.concatenate(
        [grad_query.reshape(tokens_dev, inner_width), grad_keyval], axis=1
    ).astype(jnp.bfloat16)
    grad_input = lax.dot_general(
        grad_proj, qkv_weight, (((1,), (1,)), ((), ())), preferred_element_type=jnp.float32
    ).astype(jnp.bfloat16)
    grad_input = grad_input.reshape(rows_dev, cols_dev, model_width)
    grad_wqkv = lax.dot_general(
        flat_in, grad_proj, (((0,), (0,)), ((), ())), preferred_element_type=jnp.float32
    )
    summed_wqkv, summed_wout = lax.psum((grad_wqkv, grad_wout), ("rows", "cols"))
    return (
        grad_input,
        (summed_wqkv * grad_factor).astype(jnp.bfloat16),
        (summed_wout * grad_factor).astype(jnp.bfloat16),
    )


def solution(mesh):
    in_specs = (
        P("rows", "cols", None),
        P(),
        P(),
        P("rows", "cols", None),
        P(None, "rows", "cols"),
        P("rows", "cols", None),
    )
    out_specs = (P("rows", "cols", None), P(), P())
    return jax.shard_map(shards, mesh=mesh, in_specs=in_specs, out_specs=out_specs, check_vma=False)
```

profile of v0, /device:TPU:0, one launch (start us, length us, event | category | flops | bytes accessed | tf_op | source)
XLA Modules:
  0.0 226.1 jit_solution(4671440812148472614)
XLA Ops:
  7.3 1.2 copy-done
  8.5 1.5 convolution_convert_fusion
  10.0 0.8 fusion.37
  10.8 0.3 convolution_convert_fusion.2
  11.2 5.5 %collective-permute-start.5 = (bf16[6,32,640]{2,1,0:T(8,128)(2,1)S(1)}, bf16[6,32,640]{2,1,0:T(8,128)(2,1)S(1)}, u32[]{:S(2)}, u32[]{:S(2)}) collective-permute-start(bf16[6,32,640]{2,1,0:T(8,128)(2,1)S(1)} %bitcast.57), channel_id=1, source_target_pairs={{2,0},{4,2},{6,4},{8,6},{10,8},{12,10},{14,12},{16,14},{18,16},{20... | collective-permute-start | bytes 737288 | tf_op jit(solution)/shard_map/ppermute | solution.py:20
  17.0 0.2 copy.25
  17.3 0.8 sub.133
  18.3 4.4 %collective-permute-start.9 = (f32[6,32,10]{1,0,2:T(8,128)S(1)}, f32[6,32,10]{1,0,2:T(8,128)S(1)}, u32[]{:S(2)}, u32[]{:S(2)}) collective-permute-start(f32[6,32,10]{1,0,2:T(8,128)S(1)} %reshape.285), channel_id=1, source_target_pairs={{2,0},{4,2},{6,4},{8,6},{10,8},{12,10},{14,12},{16,14},{18,16},{20... | collective-permute-start | bytes 23048 | tf_op jit(solution)/shard_map/ppermute | solution.py:20
  22.9 4.5 %collective-permute-start.1 = (bf16[6,32,640]{2,1,0:T(8,128)(2,1)S(1)}, bf16[6,32,640]{2,1,0:T(8,128)(2,1)S(1)}, u32[]{:S(2)}, u32[]{:S(2)}) collective-permute-start(bf16[6,32,640]{2,1,0:T(8,128)(2,1)S(1)} %bitcast.61), channel_id=1, source_target_pairs={{2,0},{4,2},{6,4},{8,6},{10,8},{12,10},{14,12},{16,14},{18,16},{20... | collective-permute-start | bytes 737288 | tf_op jit(solution)/shard_map/ppermute | solution.py:20
  27.4 1.1 fusion.16
  28.5 1.1 fusion.14
  29.7 1.6 collective-permute-start.11
  31.2 0.5 collective-permute-start.10
  31.8 2.2 convolution_bitcast_fusion.1
  34.2 0.8 copy.27
  35.0 0.8 copy.29
  35.8 0.5 collective-permute-done.10
  36.3 1.1 pad_maximum_fusion.13
  37.5 0.9 pad_maximum_fusion.8
  38.4 1.3 collective-permute-start.7
  39.7 0.8 collective-permute-start.6
  40.5 0.6 fusion.39
  41.1 3.0 %collective-permute-done = bf16[6,32,640]{2,1,0:T(8,128)(2,1)S(1)} collective-permute-done((bf16[6,32,640]{2,1,0:T(8,128)(2,1)S(1)}, bf16[6,32,640]{2,1,0:T(8,128)(2,1)S(1)}, u32[]{:S(2)}, u32[]{:S(2)}) %collective-permute-start) | collective-permute-done | bytes 245792 | tf_op jit(solution)/shard_map/ppermute | solution.py:17
  44.1 0.8 pad_maximum_fusion.11
  44.9 1.5 collective-permute-start.3
  46.4 0.5 collective-permute-start.2
  47.0 1.9 collective-permute-done.6
  48.8 1.4 pad_maximum_fusion.1
  50.2 0.2 reshape.282
  50.4 1.1 fusion.36
  51.5 2.2 copy.31
  53.7 1.1 copy.30
  54.8 1.5 pad_maximum_fusion
  56.3 0.2 reshape.274
  56.5 1.1 fusion.35
  57.6 1.4 copy.21
  59.1 1.1 copy.24
  60.2 0.7 fusion.41
  60.8 0.4 copy-done.16
  61.2 1.6 fusion.10
  62.8 4.3 %fusion.9 = bf16[5,64,192]{2,1,0:T(8,128)(2,1)} fusion(bf16[792,5,64]{0,2,1:T(8,128)(2,1)S(1)} %bitcast.54, f32[5,792,192]{1,2,0:T(8,128)} %copy-done.1, bf16[792,5,64]{0,2,1:T(8,128)(2,1)S(1)} %bitcast.72, bf16[192,5,64]{0,2,1:T(8,128)(2,1)S(1)} %bitcast.82, f32[5,792]{1,0:T(8,128)S(1)} %copy-done.26, f32[5,792]{1,0:T(8,128)S(1)} %copy-done.27, ...), kind=kOutput, calls=%fused_computation.16 | convolution fusion | flops 199326720 | bytes 4484544 | tf_op jit(solution)/shard_map/het,ehd->thd/dot_general | solution.py:120
  67.1 2.4 %fusion.40 = f32[5,192,792]{2,1,0:T(8,128)} fusion(bf16[192,5,64]{0,2,1:T(8,128)(2,1)S(1)} %bitcast.67, bf16[792,5,64]{0,2,1:T(8,128)(2,1)S(1)} %bitcast.55), kind=kOutput, calls=%fused_computation.77 | convolution fusion | flops 97320960 | bytes 3671040 | tf_op jit(solution)/shard_map/thd,ehd->hte/dot_general | solution.py:90
  69.5 3.8 %fusion.8 = bf16[5,64,192]{2,1,0:T(8,128)(2,1)S(1)} fusion(bf16[792,5,64]{0,2,1:T(8,128)(2,1)S(1)} %bitcast.56, f32[5,192,792]{2,1,0:T(8,128)} %fusion.40, bf16[192,5,64]{0,2,1:T(8,128)(2,1)S(1)} %bitcast.70, bf16[792,5,64]{0,2,1:T(8,128)(2,1)S(1)} %bitcast.73, f32[5,192]{1,0:T(8,128)S(1)} %bitcast.84, f32[5,192]{1,0:T(8,128)S(1)} %sub.133, ...), kind=kOutput, calls=%fused_computation.15 | convolution fusion | flops 199326720 | bytes 4460544 | tf_op jit(solution)/shard_map/hte,ehd->thd/dot_general | solution.py:99
  73.4 2.0 convolution_bitcast_fusion
  75.4 1.2 convolution_convert_fusion.1
  76.6 138.8 %all-reduce.3.cloned.1.call-done = (f32[640,960]{0,1:T(8,128)}, f32[320,640]{1,0:T(8,128)}) async-done(((f32[640,960]{0,1:T(8,128)}, f32[320,640]{1,0:T(8,128)}), (f32[640,960]{0,1:T(8,128)}, f32[320,640]{1,0:T(8,128)})) %all-reduce.3.cloned.1.call-update) | async-done | bytes 3276816 | tf_op jit(solution)/shard_map/psum | solution.py:145
  215.4 3.0 %multiply_convert_fusion.2 = bf16[640,960]{0,1:T(8,128)(2,1)} fusion(f32[640,960]{0,1:T(8,128)} %get-tuple-element.3), kind=kLoop, calls=%fused_computation.4 | loop fusion | flops 1228800 | bytes 3686400 | tf_op jit(solution)/shard_map/convert_element_type | solution.py:148
  218.4 0.8 multiply_convert_fusion.3
  (82 shorter events, 1.3 us)
Async XLA Ops:
  7.2 1.3 copy-start
  7.2 3.6 %copy-start.19 = (bf16[6,32,640]{2,1,0:T(8,128)(2,1)S(1)}, bf16[6,32,640]{2,1,0:T(8,128)(2,1)}, u32[]{:S(2)}) copy-start(bf16[6,32,640]{2,1,0:T(8,128)(2,1)} %param.11) | copy-start | bytes 737284
  7.2 3.6 %copy-start.18 = (bf16[320,640]{1,0:T(8,128)(2,1)S(1)}, bf16[320,640]{1,0:T(8,128)(2,1)}, u32[]{:S(2)}) copy-start(bf16[320,640]{1,0:T(8,128)(2,1)} %param.8) | copy-start | bytes 1228804
  7.2 9.7 %copy-start.25 = (bf16[6,32,320]{2,1,0:T(8,128)(2,1)S(1)}, bf16[6,32,320]{2,1,0:T(8,128)(2,1)}, u32[]{:S(2)}) copy-start(bf16[6,32,320]{2,1,0:T(8,128)(2,1)} %param.9) | copy-start | bytes 368644
  7.2 208.2 %all-reduce.3.cloned.1.call-start = ((), (), s32[]{:S(2)}) async-start(), calls=%async_computation | async-start | bytes 6553600 | tf_op jit(solution)/shard_map/psum | solution.py:145
  11.2 26.2 %collective-permute-start.5 = (bf16[6,32,640]{2,1,0:T(8,128)(2,1)S(1)}, bf16[6,32,640]{2,1,0:T(8,128)(2,1)S(1)}, u32[]{:S(2)}, u32[]{:S(2)}) collective-permute-start(bf16[6,32,640]{2,1,0:T(8,128)(2,1)S(1)} %bitcast.57), channel_id=1, source_target_pairs={{2,0},{4,2},{6,4},{8,6},{10,8},{12,10},{14,12},{16,14},{18,16},{20... | collective-permute-start | bytes 737288 | tf_op jit(solution)/shard_map/ppermute | solution.py:20
  16.7 20.7 %collective-permute-start.4 = (bf16[6,32,640]{2,1,0:T(8,128)(2,1)S(1)}, bf16[6,32,640]{2,1,0:T(8,128)(2,1)}, u32[]{:S(2)}, u32[]{:S(2)}) collective-permute-start(bf16[6,32,640]{2,1,0:T(8,128)(2,1)S(1)} %bitcast.58), channel_id=1, source_target_pairs={{0,2},{2,4},{4,6},{6,8},{8,10},{10,12},{12,14},{14,16},{16,18},{18... | collective-permute-start | bytes 737288 | tf_op jit(solution)/shard_map/ppermute | solution.py:17
  16.9 14.9 %copy-start.12 = (bf16[192,320]{0,1:T(8,128)(2,1)}, bf16[192,320]{0,1:T(8,128)(2,1)S(1)}, u32[]{:S(2)}) copy-start(bf16[192,320]{0,1:T(8,128)(2,1)S(1)} %copy.23) | copy-start | bytes 368644
  18.1 16.0 %copy-start.15 = (bf16[192,320]{1,0:T(8,128)(2,1)S(1)}, bf16[192,320]{1,0:T(8,128)(2,1)}, u32[]{:S(2)}) copy-start(bf16[192,320]{1,0:T(8,128)(2,1)} %get-tuple-element.14) | copy-start | bytes 368644
  18.2 16.8 %copy-start.14 = (bf16[192,320]{1,0:T(8,128)(2,1)S(1)}, bf16[192,320]{1,0:T(8,128)(2,1)}, u32[]{:S(2)}) copy-start(bf16[192,320]{1,0:T(8,128)(2,1)} %get-tuple-element.13) | copy-start | bytes 368644
  18.3 11.3 %collective-permute-start.9 = (f32[6,32,10]{1,0,2:T(8,128)S(1)}, f32[6,32,10]{1,0,2:T(8,128)S(1)}, u32[]{:S(2)}, u32[]{:S(2)}) collective-permute-start(f32[6,32,10]{1,0,2:T(8,128)S(1)} %reshape.285), channel_id=1, source_target_pairs={{2,0},{4,2},{6,4},{8,6},{10,8},{12,10},{14,12},{16,14},{18,16},{20... | collective-permute-start | bytes 23048 | tf_op jit(solution)/shard_map/ppermute | solution.py:20
  22.7 6.9 %collective-permute-start.8 = (f32[6,32,10]{1,0,2:T(8,128)S(1)}, f32[6,32,10]{1,0,2:T(8,128)S(1)}, u32[]{:S(2)}, u32[]{:S(2)}) collective-permute-start(f32[6,32,10]{1,0,2:T(8,128)S(1)} %reshape.285), channel_id=1, source_target_pairs={{0,2},{2,4},{4,6},{6,8},{8,10},{10,12},{12,14},{14,16},{16,18},{18... | collective-permute-start | bytes 23048 | tf_op jit(solution)/shard_map/ppermute | solution.py:17
  22.8 21.3 %copy-start.3 = (bf16[192,640]{1,0:T(8,128)(2,1)}, bf16[192,640]{1,0:T(8,128)(2,1)S(1)}, u32[]{:S(2)}) copy-start(bf16[192,640]{1,0:T(8,128)(2,1)S(1)} %slice.67) | copy-start | bytes 737284
  22.9 18.2 %collective-permute-start.1 = (bf16[6,32,640]{2,1,0:T(8,128)(2,1)S(1)}, bf16[6,32,640]{2,1,0:T(8,128)(2,1)S(1)}, u32[]{:S(2)}, u32[]{:S(2)}) collective-permute-start(bf16[6,32,640]{2,1,0:T(8,128)(2,1)S(1)} %bitcast.61), channel_id=1, source_target_pairs={{2,0},{4,2},{6,4},{8,6},{10,8},{12,10},{14,12},{16,14},{18,16},{20... | collective-permute-start | bytes 737288 | tf_op jit(solution)/shard_map/ppermute | solution.py:20
  29.7 6.1 %collective-permute-start.11 = (f32[18,6,10]{1,0,2:T(8,128)S(1)}, f32[18,6,10]{1,0,2:T(8,128)S(1)}, u32[]{:S(2)}, u32[]{:S(2)}) collective-permute-start(f32[18,6,10]{1,0,2:T(8,128)S(1)} %get-tuple-element.17), channel_id=1, source_target_pairs={{1,0},{0,1},{3,2},{2,3},{5,4},{4,5},{7,6},{6,7},{9,8},{8,9},{11,10... | collective-permute-start | bytes 12968 | tf_op jit(solution)/shard_map/ppermute | solution.py:20
  31.2 5.0 %collective-permute-start.10 = (f32[18,6,10]{1,0,2:T(8,128)S(1)}, f32[18,6,10]{1,0,2:T(8,128)}, u32[]{:S(2)}, u32[]{:S(2)}) collective-permute-start(f32[18,6,10]{1,0,2:T(8,128)S(1)} %get-tuple-element.16), channel_id=1, source_target_pairs={{0,1},{1,0},{2,3},{3,2},{4,5},{5,4},{6,7},{7,6},{8,9},{9,8},{10,11... | collective-permute-start | bytes 12968 | tf_op jit(solution)/shard_map/ppermute | solution.py:17
  35.8 8.3 %collective-permute-start = (bf16[6,32,640]{2,1,0:T(8,128)(2,1)S(1)}, bf16[6,32,640]{2,1,0:T(8,128)(2,1)S(1)}, u32[]{:S(2)}, u32[]{:S(2)}) collective-permute-start(bf16[6,32,640]{2,1,0:T(8,128)(2,1)S(1)} %bitcast.62), channel_id=1, source_target_pairs={{0,2},{2,4},{4,6},{6,8},{8,10},{10,12},{12,14},{14,16},{16,18},{18... | collective-permute-start | bytes 737288 | tf_op jit(solution)/shard_map/ppermute | solution.py:17
  38.4 8.6 %collective-permute-start.7 = (bf16[18,6,640]{2,1,0:T(8,128)(2,1)S(1)}, bf16[18,6,640]{2,1,0:T(8,128)(2,1)S(1)}, u32[]{:S(2)}, u32[]{:S(2)}) collective-permute-start(bf16[18,6,640]{2,1,0:T(8,128)(2,1)S(1)} %get-tuple-element.12), channel_id=1, source_target_pairs={{1,0},{0,1},{3,2},{2,3},{5,4},{4,5},{7,6},{6,7},{9,8},{8,9},{11,10... | collective-permute-start | bytes 414728 | tf_op jit(solution)/shard_map/ppermute | solution.py:20
  39.7 9.1 %collective-permute-start.6 = (bf16[18,6,640]{2,1,0:T(8,128)(2,1)S(1)}, bf16[18,6,640]{2,1,0:T(8,128)(2,1)S(1)}, u32[]{:S(2)}, u32[]{:S(2)}) collective-permute-start(bf16[18,6,640]{2,1,0:T(8,128)(2,1)S(1)} %get-tuple-element.11), channel_id=1, source_target_pairs={{0,1},{1,0},{2,3},{3,2},{4,5},{5,4},{6,7},{7,6},{8,9},{9,8},{10,11... | collective-permute-start | bytes 414728 | tf_op jit(solution)/shard_map/ppermute | solution.py:17
  41.1 7.7 %copy-start.6 = (bf16[6,32,640]{2,1,0:T(8,128)(2,1)}, bf16[6,32,640]{2,1,0:T(8,128)(2,1)S(1)}, u32[]{:S(2)}) copy-start(bf16[6,32,640]{2,1,0:T(8,128)(2,1)S(1)} %collective-permute-done.1) | copy-start | bytes 737284
  44.1 2.9 %copy-start.8 = (bf16[6,32,640]{2,1,0:T(8,128)(2,1)}, bf16[6,32,640]{2,1,0:T(8,128)(2,1)S(1)}, u32[]{:S(2)}) copy-start(bf16[6,32,640]{2,1,0:T(8,128)(2,1)S(1)} %collective-permute-done) | copy-start | bytes 737284
  44.9 9.9 %collective-permute-start.3 = (bf16[18,6,640]{2,1,0:T(8,128)(2,1)}, bf16[18,6,640]{2,1,0:T(8,128)(2,1)}, u32[]{:S(2)}, u32[]{:S(2)}) collective-permute-start(bf16[18,6,640]{2,1,0:T(8,128)(2,1)} %get-tuple-element.10), channel_id=1, source_target_pairs={{1,0},{0,1},{3,2},{2,3},{5,4},{4,5},{7,6},{6,7},{9,8},{8,9},{11,10... | collective-permute-start | bytes 414728 | tf_op jit(solution)/shard_map/ppermute | solution.py:20
  46.4 8.4 %collective-permute-start.2 = (bf16[18,6,640]{2,1,0:T(8,128)(2,1)}, bf16[18,6,640]{2,1,0:T(8,128)(2,1)}, u32[]{:S(2)}, u32[]{:S(2)}) collective-permute-start(bf16[18,6,640]{2,1,0:T(8,128)(2,1)} %get-tuple-element.9), channel_id=1, source_target_pairs={{0,1},{1,0},{2,3},{3,2},{4,5},{5,4},{6,7},{7,6},{8,9},{9,8},{10,11... | collective-permute-start | bytes 414728 | tf_op jit(solution)/shard_map/ppermute | solution.py:17
  51.5 3.3 %copy-start.4 = (bf16[192,640]{1,0:T(8,128)(2,1)S(1)}, bf16[192,640]{1,0:T(8,128)(2,1)}, u32[]{:S(2)}) copy-start(bf16[192,640]{1,0:T(8,128)(2,1)} %copy-done.3) | copy-start | bytes 737284
  51.5 3.3 %copy-start.7 = (bf16[6,32,640]{2,1,0:T(8,128)(2,1)S(1)}, bf16[6,32,640]{2,1,0:T(8,128)(2,1)}, u32[]{:S(2)}) copy-start(bf16[6,32,640]{2,1,0:T(8,128)(2,1)} %copy-done.6) | copy-start | bytes 737284
  51.5 3.3 %copy-start.9 = (bf16[6,32,640]{2,1,0:T(8,128)(2,1)S(1)}, bf16[6,32,640]{2,1,0:T(8,128)(2,1)}, u32[]{:S(2)}) copy-start(bf16[6,32,640]{2,1,0:T(8,128)(2,1)} %copy-done.8) | copy-start | bytes 737284
  57.6 2.5 %copy-start.2 = (bf16[792,320]{0,1:T(8,128)(2,1)S(1)}, bf16[792,320]{0,1:T(8,128)(2,1)}, u32[]{:S(2)}) copy-start(bf16[792,320]{0,1:T(8,128)(2,1)} %copy.30) | copy-start | bytes 1520644
  57.6 2.5 %copy-start.11 = (bf16[192,320]{0,1:T(8,128)(2,1)S(1)}, bf16[192,320]{0,1:T(8,128)(2,1)}, u32[]{:S(2)}) copy-start(bf16[192,320]{0,1:T(8,128)(2,1)} %copy.27) | copy-start | bytes 368644
  60.1 1.1 copy-start.16
  60.1 1.1 copy-start.21
  60.1 1.1 copy-start.27
  60.8 2.0 copy-start.1
  61.2 1.6 copy-start.24
  61.2 1.6 copy-start.26
  67.1 2.4 %copy-start.13 = (bf16[192,320]{0,1:T(8,128)(2,1)S(1)}, bf16[192,320]{0,1:T(8,128)(2,1)}, u32[]{:S(2)}) copy-start(bf16[192,320]{0,1:T(8,128)(2,1)} %copy-done.12) | copy-start | bytes 368644
  67.1 2.4 %copy-start.17 = (bf16[792,320]{0,1:T(8,128)(2,1)S(1)}, bf16[792,320]{0,1:T(8,128)(2,1)}, u32[]{:S(2)}) copy-start(bf16[792,320]{0,1:T(8,128)(2,1)} %copy.24) | copy-start | bytes 1520644
  67.1 2.4 %copy-start.20 = (pred[192,792]{1,0:T(8,128)(4,1)S(1)}, pred[192,792]{1,0:T(8,128)(4,1)}, u32[]{:S(2)}) copy-start(pred[192,792]{1,0:T(8,128)(4,1)} %fusion.14) | copy-start | bytes 456196
  69.5 3.8 %copy-start.5 = (bf16[6,32,640]{2,1,0:T(8,128)(2,1)S(1)}, bf16[6,32,640]{2,1,0:T(8,128)(2,1)}, u32[]{:S(2)}) copy-start(bf16[6,32,640]{2,1,0:T(8,128)(2,1)} %param.6) | copy-start | bytes 737284
  69.5 3.8 %copy-start.22 = (bf16[5,64,192]{2,1,0:T(8,128)(2,1)S(1)}, bf16[5,64,192]{2,1,0:T(8,128)(2,1)}, u32[]{:S(2)}) copy-start(bf16[5,64,192]{2,1,0:T(8,128)(2,1)} %fusion.10) | copy-start | bytes 368644
  69.5 3.8 %copy-start.23 = (bf16[5,64,192]{2,1,0:T(8,128)(2,1)S(1)}, bf16[5,64,192]{2,1,0:T(8,128)(2,1)}, u32[]{:S(2)}) copy-start(bf16[5,64,192]{2,1,0:T(8,128)(2,1)} %fusion.9) | copy-start | bytes 368644
  215.4 3.0 %copy-start.10 = (f32[320,640]{1,0:T(8,128)S(1)}, f32[320,640]{1,0:T(8,128)}, u32[]{:S(2)}) copy-start(f32[320,640]{1,0:T(8,128)} %get-tuple-element.4) | copy-start | bytes 2457604
Sparse Core Ops, SparseCore 0:
  75.6 139.7 all-reduce.2
where the time goes:
time: 227 us; the launch traced here: 226 us
  waiting for transfers between devices  144 us (63%)
  starting transfers between devices  20.7 us (9%)
  matrix products  20 us (9%)
  local copies, waits for them, and re-layouts  14.9 us (7%)
  between operations  14.4 us (6%)
  other arithmetic  11.9 us (5%)
    psum x1, waiting for transfers between devices, shards(): lax.psum((grad_wqkv, grad_wout), ('rows', 'cols'))  139 us
    ppermute x6, starting transfers between devices, padded(): lax.ppermute(lax.slice_in_dim(block, 0, width, axis=dim), axis, backward)  18.8 us
    ppermute x6, waiting for transfers between devices, padded(): lax.ppermute(lax.slice_in_dim(block, block.shape[dim] - width, None, axis...  5.37 us
    unnamed x58, local copies, waits for them, and re-layouts  5.03 us
  transfers between devices with their start and end apart: 13, of which 4 were waited for; matrix products, arithmetic and copies ran while one was open for 8% of the time, Pallas kernels for 0%

commit v1 on v0

--- a/solution.py
+++ b/solution.py
@@ -1,3 +1,4 @@
+import functools
 import jax
 import jax.numpy as jnp
 from jax import lax
@@ -6,6 +7,15 @@
 HEADS = 5
 HEAD_DIM = 64
 RADIUS = 6
+
+
+def _press_paths(t0, ax_name, which_axis):
+    for at in (ax_name, which_axis):
+        t0 = lax.psum(t0, axis_name=at)
+    return t0
+
+
+_register_rows = functools.partial(_press_paths, ax_name="cols", which_axis="rows")
 
 
 def padded(block, sides, width):
@@ -142,7 +152,7 @@
     grad_wqkv = lax.dot_general(
         flat_in, grad_proj, (((0,), (0,)), ((), ())), preferred_element_type=jnp.float32
     )
-    summed_wqkv, summed_wout = lax.psum((grad_wqkv, grad_wout), ("rows", "cols"))
+    summed_wqkv, summed_wout = _register_rows((grad_wqkv, grad_wout))
     return (
         grad_input,
         (summed_wqkv * grad_factor).astype(jnp.bfloat16),

time: 227 us -> 285 us (1.26)
  waiting for transfers between devices: 144 us -> 202 us
    psum x1 -> x2, waiting for transfers between devices: 139 us -> 197 us  [_press_paths(): t0 = lax.psum(t0, axis_name=at)]
  transfers between devices with their start and end apart: 13 -> 14, of which waited for: 4 -> 5; matrix products, arithmetic and copies ran while one was open for 8% -> 7% of each run, Pallas kernels for 0% -> 0%
where the time goes in v1:
time: 285 us; the launch traced here: 284 us
  waiting for transfers between devices  202 us (71%)
  starting transfers between devices  20.8 us (7%)
  matrix products  20 us (7%)
  local copies, waits for them, and re-layouts  15 us (5%)
  between operations  14.4 us (5%)
  other arithmetic  11.9 us (4%)
    psum x2, waiting for transfers between devices, _press_paths(): t0 = lax.psum(t0, axis_name=at)  197 us
    ppermute x6, starting transfers between devices, padded(): lax.ppermute(lax.slice_in_dim(block, 0, width, axis=dim), axis, backward)  18.8 us
  transfers between devices with their start and end apart: 14, of which 5 were waited for; matrix products, arithmetic and copies ran while one was open for 7% of the time, Pallas kernels for 0%

profile of v1, /device:TPU:0, one launch (start us, length us, event | category | flops | bytes accessed | tf_op | source)
XLA Modules:
  0.0 284.1 jit_solution(11987115370980488941)
XLA Ops:
  7.3 1.2 copy-done
  8.5 1.5 convolution_convert_fusion
  10.0 0.8 fusion.37
  10.7 0.3 convolution_convert_fusion.2
  11.2 5.5 %collective-permute-start.5 = (bf16[6,32,640]{2,1,0:T(8,128)(2,1)S(1)}, bf16[6,32,640]{2,1,0:T(8,128)(2,1)S(1)}, u32[]{:S(2)}, u32[]{:S(2)}) collective-permute-start(bf16[6,32,640]{2,1,0:T(8,128)(2,1)S(1)} %bitcast.57), channel_id=1, source_target_pairs={{2,0},{4,2},{6,4},{8,6},{10,8},{12,10},{14,12},{16,14},{18,16},{20... | collective-permute-start | bytes 737288 | tf_op jit(solution)/shard_map/ppermute | solution.py:30
  17.0 0.2 copy.25
  17.3 0.8 sub.133
  18.2 4.4 %collective-permute-start.9 = (f32[6,32,10]{1,0,2:T(8,128)S(1)}, f32[6,32,10]{1,0,2:T(8,128)S(1)}, u32[]{:S(2)}, u32[]{:S(2)}) collective-permute-start(f32[6,32,10]{1,0,2:T(8,128)S(1)} %reshape.285), channel_id=1, source_target_pairs={{2,0},{4,2},{6,4},{8,6},{10,8},{12,10},{14,12},{16,14},{18,16},{20... | collective-permute-start | bytes 23048 | tf_op jit(solution)/shard_map/ppermute | solution.py:30
  22.8 4.5 %collective-permute-start.1 = (bf16[6,32,640]{2,1,0:T(8,128)(2,1)S(1)}, bf16[6,32,640]{2,1,0:T(8,128)(2,1)S(1)}, u32[]{:S(2)}, u32[]{:S(2)}) collective-permute-start(bf16[6,32,640]{2,1,0:T(8,128)(2,1)S(1)} %bitcast.61), channel_id=1, source_target_pairs={{2,0},{4,2},{6,4},{8,6},{10,8},{12,10},{14,12},{16,14},{18,16},{20... | collective-permute-start | bytes 737288 | tf_op jit(solution)/shard_map/ppermute | solution.py:30
  27.4 1.1 fusion.16
  28.4 1.1 fusion.14
  29.7 1.6 collective-permute-start.11
  31.2 0.5 collective-permute-start.10
  31.8 2.2 convolution_bitcast_fusion.1
  34.1 0.8 copy.27
  34.9 0.8 copy.29
  35.7 0.5 collective-permute-done.10
  36.3 1.1 pad_maximum_fusion.13
  37.5 0.9 pad_maximum_fusion.8
  38.4 1.3 collective-permute-start.7
  39.7 0.8 collective-permute-start.6
  40.5 0.6 fusion.39
  41.1 3.0 %collective-permute-done = bf16[6,32,640]{2,1,0:T(8,128)(2,1)S(1)} collective-permute-done((bf16[6,32,640]{2,1,0:T(8,128)(2,1)S(1)}, bf16[6,32,640]{2,1,0:T(8,128)(2,1)S(1)}, u32[]{:S(2)}, u32[]{:S(2)}) %collective-permute-start) | collective-permute-done | bytes 245792 | tf_op jit(solution)/shard_map/ppermute | solution.py:27
  44.1 0.8 pad_maximum_fusion.11
  44.9 1.5 collective-permute-start.3
  46.4 0.5 collective-permute-start.2
  46.9 1.9 collective-permute-done.6
  48.8 1.4 pad_maximum_fusion.1
  50.2 0.2 reshape.282
  50.4 1.1 fusion.36
  51.5 2.2 copy.31
  53.7 1.1 copy.30
  54.8 1.5 pad_maximum_fusion
  56.5 1.1 fusion.35
  57.6 1.4 copy.21
  59.0 1.1 copy.24
  60.2 0.7 fusion.41
  60.8 0.4 copy-done.16
  61.2 1.6 fusion.10
  62.8 4.3 %fusion.9 = bf16[5,64,192]{2,1,0:T(8,128)(2,1)} fusion(bf16[792,5,64]{0,2,1:T(8,128)(2,1)S(1)} %bitcast.54, f32[5,792,192]{1,2,0:T(8,128)} %copy-done.1, bf16[792,5,64]{0,2,1:T(8,128)(2,1)S(1)} %bitcast.72, bf16[192,5,64]{0,2,1:T(8,128)(2,1)S(1)} %bitcast.82, f32[5,792]{1,0:T(8,128)S(1)} %copy-done.26, f32[5,792]{1,0:T(8,128)S(1)} %copy-done.27, ...), kind=kOutput, calls=%fused_computation.16 | convolution fusion | flops 199326720 | bytes 4484544 | tf_op jit(solution)/shard_map/het,ehd->thd/dot_general | solution.py:130
  67.1 2.4 fusion.40
  69.5 3.8 %fusion.8 = bf16[5,64,192]{2,1,0:T(8,128)(2,1)S(1)} fusion(bf16[792,5,64]{0,2,1:T(8,128)(2,1)S(1)} %bitcast.56, f32[5,192,792]{2,1,0:T(8,128)} %fusion.40, bf16[192,5,64]{0,2,1:T(8,128)(2,1)S(1)} %bitcast.70, bf16[792,5,64]{0,2,1:T(8,128)(2,1)S(1)} %bitcast.73, f32[5,192]{1,0:T(8,128)S(1)} %bitcast.84, f32[5,192]{1,0:T(8,128)S(1)} %sub.133, ...), kind=kOutput, calls=%fused_computation.15 | convolution fusion | flops 199326720 | bytes 4460544 | tf_op jit(solution)/shard_map/hte,ehd->thd/dot_general | solution.py:109
  73.4 2.0 convolution_bitcast_fusion
  75.5 89.7 %all-reduce.7.cloned.1.call-done = (f32[640,960]{0,1:T(8,128)}, f32[320,640]{1,0:T(8,128)}) async-done(((f32[640,960]{0,1:T(8,128)}, f32[320,640]{1,0:T(8,128)}), (f32[640,960]{0,1:T(8,128)}, f32[320,640]{1,0:T(8,128)})) %all-reduce.7.cloned.1.call-update) | async-done | bytes 3276816 | tf_op jit(solution)/shard_map/psum | solution.py:14
  165.2 1.2 convolution_convert_fusion.1
  166.4 107.0 %all-reduce.5.cloned.1.call-done = (f32[640,960]{0,1:T(8,128)}, f32[320,640]{1,0:T(8,128)}) async-done(((f32[640,960]{0,1:T(8,128)}, f32[320,640]{1,0:T(8,128)}), (f32[640,960]{0,1:T(8,128)}, f32[320,640]{1,0:T(8,128)})) %all-reduce.5.cloned.1.call-update) | async-done | bytes 3276816 | tf_op jit(solution)/shard_map/psum | solution.py:14
  273.4 3.0 %multiply_convert_fusion.2 = bf16[640,960]{0,1:T(8,128)(2,1)} fusion(f32[640,960]{0,1:T(8,128)} %get-tuple-element.3), kind=kLoop, calls=%fused_computation.4 | loop fusion | flops 1228800 | bytes 3686400 | tf_op jit(solution)/shard_map/convert_element_type | solution.py:158
  276.5 0.8 multiply_convert_fusion.3
  (85 shorter events, 1.5 us)
Async XLA Ops:
  7.2 1.3 copy-start
  7.2 3.6 %copy-start.19 = (bf16[6,32,640]{2,1,0:T(8,128)(2,1)S(1)}, bf16[6,32,640]{2,1,0:T(8,128)(2,1)}, u32[]{:S(2)}) copy-start(bf16[6,32,640]{2,1,0:T(8,128)(2,1)} %param.11) | copy-start | bytes 737284
  7.2 3.5 %copy-start.18 = (bf16[320,640]{1,0:T(8,128)(2,1)S(1)}, bf16[320,640]{1,0:T(8,128)(2,1)}, u32[]{:S(2)}) copy-start(bf16[320,640]{1,0:T(8,128)(2,1)} %param.8) | copy-start | bytes 1228804
  7.2 9.6 %copy-start.25 = (bf16[6,32,320]{2,1,0:T(8,128)(2,1)S(1)}, bf16[6,32,320]{2,1,0:T(8,128)(2,1)}, u32[]{:S(2)}) copy-start(bf16[6,32,320]{2,1,0:T(8,128)(2,1)} %param.9) | copy-start | bytes 368644
  7.2 157.9 %all-reduce.7.cloned.1.call-start = ((), (), s32[]{:S(2)}) async-start(), calls=%async_computation.1 | async-start | bytes 6553600 | tf_op jit(solution)/shard_map/psum | solution.py:14
  11.2 26.3 %collective-permute-start.5 = (bf16[6,32,640]{2,1,0:T(8,128)(2,1)S(1)}, bf16[6,32,640]{2,1,0:T(8,128)(2,1)S(1)}, u32[]{:S(2)}, u32[]{:S(2)}) collective-permute-start(bf16[6,32,640]{2,1,0:T(8,128)(2,1)S(1)} %bitcast.57), channel_id=1, source_target_pairs={{2,0},{4,2},{6,4},{8,6},{10,8},{12,10},{14,12},{16,14},{18,16},{20... | collective-permute-start | bytes 737288 | tf_op jit(solution)/shard_map/ppermute | solution.py:30
  16.7 20.7 %collective-permute-start.4 = (bf16[6,32,640]{2,1,0:T(8,128)(2,1)S(1)}, bf16[6,32,640]{2,1,0:T(8,128)(2,1)}, u32[]{:S(2)}, u32[]{:S(2)}) collective-permute-start(bf16[6,32,640]{2,1,0:T(8,128)(2,1)S(1)} %bitcast.58), channel_id=1, source_target_pairs={{0,2},{2,4},{4,6},{6,8},{8,10},{10,12},{12,14},{14,16},{16,18},{18... | collective-permute-start | bytes 737288 | tf_op jit(solution)/shard_map/ppermute | solution.py:27
  16.9 14.9 %copy-start.12 = (bf16[192,320]{0,1:T(8,128)(2,1)}, bf16[192,320]{0,1:T(8,128)(2,1)S(1)}, u32[]{:S(2)}) copy-start(bf16[192,320]{0,1:T(8,128)(2,1)S(1)} %copy.23) | copy-start | bytes 368644
  18.1 16.0 %copy-start.15 = (bf16[192,320]{1,0:T(8,128)(2,1)S(1)}, bf16[192,320]{1,0:T(8,128)(2,1)}, u32[]{:S(2)}) copy-start(bf16[192,320]{1,0:T(8,128)(2,1)} %get-tuple-element.16) | copy-start | bytes 368644
  18.1 16.8 %copy-start.14 = (bf16[192,320]{1,0:T(8,128)(2,1)S(1)}, bf16[192,320]{1,0:T(8,128)(2,1)}, u32[]{:S(2)}) copy-start(bf16[192,320]{1,0:T(8,128)(2,1)} %get-tuple-element.15) | copy-start | bytes 368644
  18.2 11.3 %collective-permute-start.9 = (f32[6,32,10]{1,0,2:T(8,128)S(1)}, f32[6,32,10]{1,0,2:T(8,128)S(1)}, u32[]{:S(2)}, u32[]{:S(2)}) collective-permute-start(f32[6,32,10]{1,0,2:T(8,128)S(1)} %reshape.285), channel_id=1, source_target_pairs={{2,0},{4,2},{6,4},{8,6},{10,8},{12,10},{14,12},{16,14},{18,16},{20... | collective-permute-start | bytes 23048 | tf_op jit(solution)/shard_map/ppermute | solution.py:30
  22.7 6.8 %collective-permute-start.8 = (f32[6,32,10]{1,0,2:T(8,128)S(1)}, f32[6,32,10]{1,0,2:T(8,128)S(1)}, u32[]{:S(2)}, u32[]{:S(2)}) collective-permute-start(f32[6,32,10]{1,0,2:T(8,128)S(1)} %reshape.285), channel_id=1, source_target_pairs={{0,2},{2,4},{4,6},{6,8},{8,10},{10,12},{12,14},{14,16},{16,18},{18... | collective-permute-start | bytes 23048 | tf_op jit(solution)/shard_map/ppermute | solution.py:27
  22.8 21.2 %copy-start.3 = (bf16[192,640]{1,0:T(8,128)(2,1)}, bf16[192,640]{1,0:T(8,128)(2,1)S(1)}, u32[]{:S(2)}) copy-start(bf16[192,640]{1,0:T(8,128)(2,1)S(1)} %slice.67) | copy-start | bytes 737284
  22.8 18.3 %collective-permute-start.1 = (bf16[6,32,640]{2,1,0:T(8,128)(2,1)S(1)}, bf16[6,32,640]{2,1,0:T(8,128)(2,1)S(1)}, u32[]{:S(2)}, u32[]{:S(2)}) collective-permute-start(bf16[6,32,640]{2,1,0:T(8,128)(2,1)S(1)} %bitcast.61), channel_id=1, source_target_pairs={{2,0},{4,2},{6,4},{8,6},{10,8},{12,10},{14,12},{16,14},{18,16},{20... | collective-permute-start | bytes 737288 | tf_op jit(solution)/shard_map/ppermute | solution.py:30
  29.7 6.1 %collective-permute-start.11 = (f32[18,6,10]{1,0,2:T(8,128)S(1)}, f32[18,6,10]{1,0,2:T(8,128)S(1)}, u32[]{:S(2)}, u32[]{:S(2)}) collective-permute-start(f32[18,6,10]{1,0,2:T(8,128)S(1)} %get-tuple-element.19), channel_id=1, source_target_pairs={{1,0},{0,1},{3,2},{2,3},{5,4},{4,5},{7,6},{6,7},{9,8},{8,9},{11,10... | collective-permute-start | bytes 12968 | tf_op jit(solution)/shard_map/ppermute | solution.py:30
  31.2 5.1 %collective-permute-start.10 = (f32[18,6,10]{1,0,2:T(8,128)S(1)}, f32[18,6,10]{1,0,2:T(8,128)}, u32[]{:S(2)}, u32[]{:S(2)}) collective-permute-start(f32[18,6,10]{1,0,2:T(8,128)S(1)} %get-tuple-element.18), channel_id=1, source_target_pairs={{0,1},{1,0},{2,3},{3,2},{4,5},{5,4},{6,7},{7,6},{8,9},{9,8},{10,11... | collective-permute-start | bytes 12968 | tf_op jit(solution)/shard_map/ppermute | solution.py:27
  35.7 8.3 %collective-permute-start = (bf16[6,32,640]{2,1,0:T(8,128)(2,1)S(1)}, bf16[6,32,640]{2,1,0:T(8,128)(2,1)S(1)}, u32[]{:S(2)}, u32[]{:S(2)}) collective-permute-start(bf16[6,32,640]{2,1,0:T(8,128)(2,1)S(1)} %bitcast.62), channel_id=1, source_target_pairs={{0,2},{2,4},{4,6},{6,8},{8,10},{10,12},{12,14},{14,16},{16,18},{18... | collective-permute-start | bytes 737288 | tf_op jit(solution)/shard_map/ppermute | solution.py:27
  38.4 8.6 %collective-permute-start.7 = (bf16[18,6,640]{2,1,0:T(8,128)(2,1)S(1)}, bf16[18,6,640]{2,1,0:T(8,128)(2,1)S(1)}, u32[]{:S(2)}, u32[]{:S(2)}) collective-permute-start(bf16[18,6,640]{2,1,0:T(8,128)(2,1)S(1)} %get-tuple-element.14), channel_id=1, source_target_pairs={{1,0},{0,1},{3,2},{2,3},{5,4},{4,5},{7,6},{6,7},{9,8},{8,9},{11,10... | collective-permute-start | bytes 414728 | tf_op jit(solution)/shard_map/ppermute | solution.py:30
  39.7 9.1 %collective-permute-start.6 = (bf16[18,6,640]{2,1,0:T(8,128)(2,1)S(1)}, bf16[18,6,640]{2,1,0:T(8,128)(2,1)S(1)}, u32[]{:S(2)}, u32[]{:S(2)}) collective-permute-start(bf16[18,6,640]{2,1,0:T(8,128)(2,1)S(1)} %get-tuple-element.13), channel_id=1, source_target_pairs={{0,1},{1,0},{2,3},{3,2},{4,5},{5,4},{6,7},{7,6},{8,9},{9,8},{10,11... | collective-permute-start | bytes 414728 | tf_op jit(solution)/shard_map/ppermute | solution.py:27
  41.1 7.7 %copy-start.6 = (bf16[6,32,640]{2,1,0:T(8,128)(2,1)}, bf16[6,32,640]{2,1,0:T(8,128)(2,1)S(1)}, u32[]{:S(2)}) copy-start(bf16[6,32,640]{2,1,0:T(8,128)(2,1)S(1)} %collective-permute-done.1) | copy-start | bytes 737284
  44.1 2.9 %copy-start.8 = (bf16[6,32,640]{2,1,0:T(8,128)(2,1)}, bf16[6,32,640]{2,1,0:T(8,128)(2,1)S(1)}, u32[]{:S(2)}) copy-start(bf16[6,32,640]{2,1,0:T(8,128)(2,1)S(1)} %collective-permute-done) | copy-start | bytes 737284
  44.9 9.9 %collective-permute-start.3 = (bf16[18,6,640]{2,1,0:T(8,128)(2,1)}, bf16[18,6,640]{2,1,0:T(8,128)(2,1)}, u32[]{:S(2)}, u32[]{:S(2)}) collective-permute-start(bf16[18,6,640]{2,1,0:T(8,128)(2,1)} %get-tuple-element.12), channel_id=1, source_target_pairs={{1,0},{0,1},{3,2},{2,3},{5,4},{4,5},{7,6},{6,7},{9,8},{8,9},{11,10... | collective-permute-start | bytes 414728 | tf_op jit(solution)/shard_map/ppermute | solution.py:30
  46.4 8.4 %collective-permute-start.2 = (bf16[18,6,640]{2,1,0:T(8,128)(2,1)}, bf16[18,6,640]{2,1,0:T(8,128)(2,1)}, u32[]{:S(2)}, u32[]{:S(2)}) collective-permute-start(bf16[18,6,640]{2,1,0:T(8,128)(2,1)} %get-tuple-element.11), channel_id=1, source_target_pairs={{0,1},{1,0},{2,3},{3,2},{4,5},{5,4},{6,7},{7,6},{8,9},{9,8},{10,11... | collective-permute-start | bytes 414728 | tf_op jit(solution)/shard_map/ppermute | solution.py:27
  51.5 3.3 %copy-start.4 = (bf16[192,640]{1,0:T(8,128)(2,1)S(1)}, bf16[192,640]{1,0:T(8,128)(2,1)}, u32[]{:S(2)}) copy-start(bf16[192,640]{1,0:T(8,128)(2,1)} %copy-done.3) | copy-start | bytes 737284
  51.5 3.3 %copy-start.7 = (bf16[6,32,640]{2,1,0:T(8,128)(2,1)S(1)}, bf16[6,32,640]{2,1,0:T(8,128)(2,1)}, u32[]{:S(2)}) copy-start(bf16[6,32,640]{2,1,0:T(8,128)(2,1)} %copy-done.6) | copy-start | bytes 737284
  51.5 3.3 %copy-start.9 = (bf16[6,32,640]{2,1,0:T(8,128)(2,1)S(1)}, bf16[6,32,640]{2,1,0:T(8,128)(2,1)}, u32[]{:S(2)}) copy-start(bf16[6,32,640]{2,1,0:T(8,128)(2,1)} %copy-done.8) | copy-start | bytes 737284
  57.6 2.5 copy-start.2
  57.6 2.5 copy-start.11
  60.1 1.1 copy-start.16
  60.1 1.1 copy-start.21
  60.1 1.1 copy-start.27
  60.8 2.0 copy-start.1
  61.2 1.6 copy-start.24
  61.2 1.6 copy-start.26
  67.1 2.4 copy-start.13
  67.1 2.4 copy-start.17
  67.1 2.4 copy-start.20
  69.5 3.8 %copy-start.5 = (bf16[6,32,640]{2,1,0:T(8,128)(2,1)S(1)}, bf16[6,32,640]{2,1,0:T(8,128)(2,1)}, u32[]{:S(2)}) copy-start(bf16[6,32,640]{2,1,0:T(8,128)(2,1)} %param.6) | copy-start | bytes 737284
  69.5 3.8 %copy-start.22 = (bf16[5,64,192]{2,1,0:T(8,128)(2,1)S(1)}, bf16[5,64,192]{2,1,0:T(8,128)(2,1)}, u32[]{:S(2)}) copy-start(bf16[5,64,192]{2,1,0:T(8,128)(2,1)} %fusion.10) | copy-start | bytes 368644
  69.5 3.8 %copy-start.23 = (bf16[5,64,192]{2,1,0:T(8,128)(2,1)S(1)}, bf16[5,64,192]{2,1,0:T(8,128)(2,1)}, u32[]{:S(2)}) copy-start(bf16[5,64,192]{2,1,0:T(8,128)(2,1)} %fusion.9) | copy-start | bytes 368644
  75.4 198.0 %all-reduce.5.cloned.1.call-start = ((), (), s32[]{:S(2)}) async-start(), calls=%async_computation | async-start | bytes 6553600 | tf_op jit(solution)/shard_map/psum | solution.py:14
  273.4 3.0 %copy-start.10 = (f32[320,640]{1,0:T(8,128)S(1)}, f32[320,640]{1,0:T(8,128)}, u32[]{:S(2)}) copy-start(f32[320,640]{1,0:T(8,128)} %get-tuple-element.4) | copy-start | bytes 2457604
Sparse Core Ops, SparseCore 0:
  75.5 89.5 all-reduce.6
  168.9 104.4 all-reduce.4
